TPU v7x, 256 devices: a whole 4x4x8 slice. The times are simulated.
256 devices in a mesh: grp: 4 (over z_hi, core), sub: 64 (over y, z_lo, x).
Axes of the slice: x: 4, y: 4, z: 8 (z_hi: 2, z_lo: 4; z = z_hi * 4 + z_lo), core: 2. Of those that a mesh axis runs over, the one named last changes fastest.
Arguments:
- operators: float32 [4, 64, 4, 512, 512], P('grp', 'sub'), may hold values from -1 to 6
- counts: int32 [4, 64], P('grp', 'sub'), may hold values from 1 to 4, as said below
- pair_rows: int32 [4, 64, 4, 256], P('grp', 'sub'), may hold values from -256 to 256, as said below
- gap: float32 [4, 64, 4, 256, 128], P('grp', 'sub'), may hold values from -6 to 6
Outputs:
- multipliers: float32 [4, 64, 4, 256, 128], P('grp', 'sub')
- residual: float32 [4, 64, 4, 256, 128], P('grp', 'sub')
Inputs may be any that keep to these rules, and one draw needn't show every extreme that they name: `counts`: each group has at least one owner with 4 subdomains. `pair_rows`: for each group, owner and slot the absolute values are a permutation of 1 to 256.
All inputs are finite; a program needn't handle non-finite values.
Results may differ from a plain program's by a relative error of at most 0.00022.
Values sent between devices are 32-bit elements; how exact they have to be, the bound alone decides.
A program may use at most 64 MiB of HBM per device.

v0:
```python
import functools

import jax
import jax.numpy as jnp
from jax import lax
from jax.experimental import pallas as pl
from jax.experimental.pallas import tpu as pltpu
from jax.sharding import PartitionSpec as P

M = 512
H = 256
RHS = 128
SLOTS = 4
ITERS = 6
CHUNKS = 2
W = RHS // CHUNKS
STEPS = (ITERS + 1) * CHUNKS

LOWER = 1.0
UPPER = 14.0
CENTRE = (UPPER + LOWER) / 2.0
RADIUS = (UPPER - LOWER) / 2.0

F32 = jnp.float32
BF16 = jnp.bfloat16


def coefficients():
    spread = CENTRE / RADIUS
    rho = 1.0 / spread
    keep, add = {1: 0.0}, {1: 1.0 / CENTRE}
    for t in range(2, ITERS + 1):
        new = 1.0 / (2.0 * spread - rho)
        keep[t] = new * rho
        add[t] = 2.0 * new / RADIUS
        rho = new
    return keep, add


KEEP, ADD = coefficients()


def chosen(table, t):
    value = jnp.float32(table[ITERS])
    for k in range(1, ITERS):
        value = jnp.where(t == k, jnp.float32(table[k]), value)
    return value


def halves(x):
    high = x.astype(BF16)
    low = (x - high.astype(F32)).astype(BF16)
    return high, low


def nn(a, b):
    return jnp.dot(a, b, preferred_element_type=F32)


def nt(a, b):
    return lax.dot_general(a, b, (((1,), (1,)), ((), ())), preferred_element_type=F32)


def product(x, w):
    both = nn(x, w[0])
    return (both[:W] + both[W:]) + nn(x[:W], w[1])


def kernel(far, cnt_ref, pairs_ref, ops_hbm, gap_hbm, out_x, out_r,
           ops, gap, w_in, w_p, w_ll, w_lr, w_far, vb, vp, v_ghost, r_ghost, v_end, r_end, x_end, v_in, r_in, x_in, own,
           p_out, p_got, q_out, q_got, ll_out, ll_got,
           load_sem, gap_sem, ll_sem, p_send, p_recv, q_send, q_recv):
    s = lax.axis_index("sub")
    has_left = s > 0
    has_right = s < lax.axis_size("sub") - 1
    c = cnt_ref[0, 0]
    final_slot = jnp.clip(c - 1, 0, SLOTS - 1)

    gap_load = pltpu.make_async_copy(gap_hbm.at[0, 0], gap, gap_sem)
    gap_load.start()
    loads = [pltpu.make_async_copy(ops_hbm.at[0, 0, j], ops.at[j], load_sem.at[j]) for j in range(SLOTS)]
    for load in loads:
        load.start()

    barrier = pltpu.get_barrier_semaphore()

    @pl.when(has_left)
    def _():
        pl.semaphore_signal(barrier, inc=1, device_id={"sub": s - 1}, device_id_type=pl.DeviceIdType.MESH)

    @pl.when(has_right)
    def _():
        pl.semaphore_signal(barrier, inc=1, device_id={"sub": s + 1}, device_id_type=pl.DeviceIdType.MESH)

    @pl.when(jnp.logical_not(has_left))
    def _():
        p_got[...] = jnp.zeros_like(p_got)

    @pl.when(jnp.logical_not(has_right))
    def _():
        q_got[...] = jnp.zeros_like(q_got)

    for ref in (v_ghost, r_ghost, v_end, r_end, x_end, own, x_in, vp, w_far):
        ref[...] = jnp.zeros_like(ref)
    q_out[0] = jnp.zeros(q_out.shape[1:], F32)
    q_got[0] = jnp.zeros(q_got.shape[1:], F32)

    def p_copy(t, h):
        return pltpu.make_async_remote_copy(
            src_ref=p_out.at[t, h], dst_ref=p_got.at[t, h], send_sem=p_send.at[h], recv_sem=p_recv.at[t, h],
            device_id={"sub": s + 1}, device_id_type=pl.DeviceIdType.MESH)

    def q_copy(t, h):
        return pltpu.make_async_remote_copy(
            src_ref=q_out.at[t, h], dst_ref=q_got.at[t, h], send_sem=q_send.at[h], recv_sem=q_recv.at[t, h],
            device_id={"sub": s - 1}, device_id_type=pl.DeviceIdType.MESH)

    ll_copy = pltpu.make_async_remote_copy(
        src_ref=ll_out, dst_ref=ll_got, send_sem=ll_sem.at[0], recv_sem=ll_sem.at[1],
        device_id={"sub": s - 1}, device_id_type=pl.DeviceIdType.MESH)

    gap_load.wait()
    top = jnp.where(has_right, jnp.transpose(gap[final_slot]), 0.0)
    for h in range(CHUNKS):
        p_out[0, h] = -top[h * W:(h + 1) * W]
    for j in range(SLOTS - 1):
        turned_gap = jnp.where(j < c - 1, jnp.transpose(gap[j]), 0.0)
        for h in range(CHUNKS):
            r = turned_gap[h * W:(h + 1) * W]
            r_in[h, j] = r
            v_in[h, j] = r * (1.0 / CENTRE)

    rows = lax.broadcasted_iota(jnp.int32, (H, H), 0)
    columns = lax.broadcasted_iota(jnp.int32, (H, H), 1)
    unit = jnp.where(rows == columns, 1.0, 0.0).astype(BF16)

    def selection(pairs):
        sign = jnp.where(pairs > 0, -1.0, 1.0)
        return jnp.where(rows == jnp.abs(pairs) - 1, sign, 0.0).astype(BF16)

    def turned(picked, block):
        high, low = halves(block)
        return nt(picked, high).astype(BF16), nt(picked, low).astype(BF16)

    def left_left(picked, j):
        high, low = turned(picked, ops[j, :H, :H])
        return nt(high, picked), nt(low, picked)

    def left_right(picked, j):
        high, low = halves(ops[j, :H, H:])
        return (nt(unit, nn(picked, high).astype(BF16)).astype(BF16),
                nt(unit, nn(picked, low).astype(BF16)).astype(BF16))

    pairs = [pairs_ref[0, 0, j:j + 1, :] for j in range(SLOTS)]
    loads[0].wait()
    picked = selection(pairs[0])
    ll_high, ll_low = left_left(picked, 0)
    ll_out[...] = ll_high + ll_low
    w_ll[0] = ll_high.astype(BF16)
    w_ll[1] = ll_low.astype(BF16)
    w_lr[0], w_lr[1] = left_right(picked, 0)

    for load in loads[1:]:
        load.wait()
    last_pairs = jnp.where(c == 1, pairs[0], jnp.where(c == 2, pairs[1], jnp.where(c == 3, pairs[2], pairs[3])))
    w_p[0, :H], w_p[1, :H] = turned(selection(last_pairs), ops[final_slot, H:, :H])
    w_p[0, H:], w_p[1, H:] = turned(unit, ops[final_slot, H:, H:])

    pl.semaphore_wait(barrier, has_left.astype(jnp.int32) + has_right.astype(jnp.int32))

    @pl.when(has_right)
    def _():
        for h in range(CHUNKS):
            p_copy(0, h).start()

    @pl.when(has_left)
    def _():
        ll_copy.start()

    def end_step(n):
        t, h = n // CHUNKS + 1, n % CHUNKS
        keep, add = chosen(KEEP, t), chosen(ADD, t)

        @pl.when(jnp.logical_and(has_right, n == CHUNKS))
        def _():
            ll_copy.wait_recv()
            w_far[0], w_far[1] = halves(ll_got[...])

        partial = p_out[t - 1, h] + product(vp[h, :, H:], w_far)

        @pl.when(jnp.logical_and(has_right, t > 1))
        def _():
            q_copy(t - 1, h).wait_recv()

        r = r_end[h] - jnp.where(has_right, partial + q_got[t - 1, h], 0.0)
        r_end[h] = r

        @pl.when(t <= ITERS)
        def _():
            end = keep * v_end[h] + add * r
            v_end[h] = end
            x_end[h] = x_end[h] + end
            high, low = halves(end)
            vp[h, :W, H:] = high
            vp[h, W:, H:] = low
            high, low = halves(jnp.where(c == 1, end, v_in[h, 0]))
            vb[h, :W, H:2 * H] = high
            vb[h, W:, H:2 * H] = low

            @pl.when(jnp.logical_and(has_left, t > 1))
            def _():
                q_copy(t - 1, h).wait_send()

            q_out[t, h] = product(vb[h, :, H:2 * H], w_lr)

            @pl.when(has_left)
            def _():
                q_copy(t, h).start()

    def ghost_step(n):
        t, h = n // CHUNKS + 1, n % CHUNKS
        keep, add = chosen(KEEP, t), chosen(ADD, t)
        keep_next, add_next = chosen(KEEP, t + 1), chosen(ADD, t + 1)
        partial = q_out[t - 1, h] + own[h]

        @pl.when(has_left)
        def _():
            p_copy(t - 1, h).wait_recv()

        r = r_ghost[h] - jnp.where(has_left, partial + p_got[t - 1, h], 0.0)
        ghost = keep * v_ghost[h] + add * r
        r_ghost[h] = r
        v_ghost[h] = ghost
        inner = [v_in[h, j] for j in range(3)]
        end = v_end[h]
        before = jnp.where(c == 1, ghost, jnp.where(c == 2, inner[0], jnp.where(c == 3, inner[1], inner[2])))
        high, low = halves(before)
        vp[h, :W, :H] = high
        vp[h, W:, :H] = low
        blocks = {0: ghost, 2: jnp.where(c == 2, end, inner[1]), 3: jnp.where(c == 3, end, inner[2]), 4: end}
        for i, block in blocks.items():
            high, low = halves(block)
            vb[h, :W, i * H:(i + 1) * H] = high
            vb[h, W:, i * H:(i + 1) * H] = low

        @pl.when(has_right)
        def _():
            p_copy(t - 1, h).wait_send()

        p_out[t, h] = product(vp[h], w_p)

        @pl.when(jnp.logical_and(has_right, t < ITERS))
        def _():
            p_copy(t, h).start()

        for j in range(3):
            y = product(vb[h, :, j * H:(j + 3) * H], w_in.at[j])
            r = r_in[h, j] - jnp.where(j < c - 1, y, 0.0)
            r_in[h, j] = r
            x_in[h, j] = x_in[h, j] + inner[j]
            v_in[h, j] = keep_next * inner[j] + add_next * r
        own[h] = product(vb[h, :, :H], w_ll)

    ahead = jnp.where(s % far == 0, CHUNKS, 1)

    @pl.loop(0, ahead)
    def _(n):
        end_step(n)

    for j in range(SLOTS):
        picked = selection(pairs[j])
        if j > 0:
            ll_high, ll_low = left_left(picked, j)
            rr_high, rr_low = turned(unit, ops[j - 1, H:, H:])
            mid_high, mid_low = halves((rr_high.astype(F32) + ll_high) + (rr_low.astype(F32) + ll_low))
            w_in[j - 1, 0, H:2 * H] = mid_high
            w_in[j - 1, 1, H:2 * H] = mid_low
            w_in[j - 1, 0, 2 * H:], w_in[j - 1, 1, 2 * H:] = left_right(picked, j)
        if j < SLOTS - 1:
            w_in[j, 0, :H], w_in[j, 1, :H] = turned(picked, ops[j, H:, :H])

    def placed(inner, end, j):
        kept = jnp.where(j < c - 1, inner, 0.0) if j < 3 else jnp.zeros_like(end)
        return jnp.transpose(jnp.where(c - 1 == j, end, kept))

    @pl.loop(0, ITERS * CHUNKS)
    def _(n):
        ghost_step(n)

        @pl.when(n == ITERS * CHUNKS - 1)
        def _():
            end = x_end[...].reshape(RHS, H)
            for j in range(SLOTS):
                out_x[0, 0, j] = placed(x_in[:, j % 3].reshape(RHS, H), end, j)
                out_r[0, 0, j] = placed(r_in[:, j % 3].reshape(RHS, H), jnp.zeros_like(end), j)

        end_step(n + ahead)

    @pl.loop(ITERS * CHUNKS + ahead, STEPS)
    def _(n):
        end_step(n)

    end = jnp.transpose(r_end[...].reshape(RHS, H))
    for j in range(SLOTS):
        out_r[0, 0, j] = jnp.where(c - 1 == j, end, out_r[0, 0, j])

    @pl.when(has_left)
    def _():
        ll_copy.wait_send()
        for h in range(CHUNKS):
            q_copy(ITERS, h).wait_send()


def shards(far, operators, counts, pair_rows, gap):
    hbm = pl.BlockSpec(memory_space=pltpu.HBM)
    vmem = pl.BlockSpec(memory_space=pltpu.VMEM)
    dma = pltpu.SemaphoreType.DMA
    message = pltpu.VMEM((ITERS + 1, CHUNKS, W, H), F32)
    chunk = pltpu.VMEM((CHUNKS, W, H), F32)
    inner = pltpu.VMEM((CHUNKS, 3, W, H), F32)
    operator = pltpu.VMEM((2, H, H), BF16)
    block = jax.ShapeDtypeStruct((1, 1, SLOTS, H, RHS), F32)
    return pl.pallas_call(
        functools.partial(kernel, far),
        out_shape=(block, block),
        in_specs=[pl.BlockSpec(memory_space=pltpu.SMEM), vmem, hbm, hbm],
        out_specs=(vmem, vmem),
        scratch_shapes=[
            pltpu.VMEM((SLOTS, M, M), F32),
            pltpu.VMEM((SLOTS, H, RHS), F32),
            pltpu.VMEM((3, 2, 3 * H, H), BF16),
            pltpu.VMEM((2, 2 * H, H), BF16),
            operator,
            operator,
            operator,
            pltpu.VMEM((CHUNKS, 2 * W, 5 * H), BF16),
            pltpu.VMEM((CHUNKS, 2 * W, 2 * H), BF16),
            chunk, chunk, chunk, chunk, chunk,
            inner, inner, inner,
            chunk,
            message, message, message, message,
            pltpu.VMEM((H, H), F32),
            pltpu.VMEM((H, H), F32),
            dma((SLOTS,)),
            dma,
            dma((2,)),
            dma((CHUNKS,)),
            dma((ITERS + 1, CHUNKS)),
            dma((CHUNKS,)),
            dma((ITERS + 1, CHUNKS)),
        ],
        compiler_params=pltpu.CompilerParams(
            collective_id=0, has_side_effects=True, vmem_limit_bytes=65_798_144),
        name="feti_chebyshev",
    )(counts, pair_rows, operators, gap)


def solution(mesh):
    return jax.shard_map(
        functools.partial(shards, 16 if mesh.shape["sub"] % 16 == 0 else 2),
        mesh=mesh,
        in_specs=(
            P("grp", "sub", None, None, None),
            P("grp", "sub"),
            P("grp", "sub", None, None),
            P("grp", "sub", None, None, None),
        ),
        out_specs=(P("grp", "sub", None, None, None), P("grp", "sub", None, None, None)),
        check_vma=False,
    )
```

profile of v0, /device:TPU:24, one launch (start us, length us, event | category | flops | bytes accessed | tf_op | source)
XLA Modules:
  0.0 50.4 jit_solution(8491506242798351261)
XLA Ops:
  1.3 45.4 %feti_chebyshev.1 = (f32[1,1,4,256,128]{4,3,2,1,0:T(8,128)}, f32[1,1,4,256,128]{4,3,2,1,0:T(8,128)}) custom-call(s32[1,1]{1,0:T(1,128)S(6)} %copy.8.cnt_ref, s32[1,1,4,256]{3,2,1,0:T(4,128)} %pairs_ref.1, f32[1,1,4,512,512]{4,3,2,1,0:T(8,128)} %ops_hbm.1, f32[1,1,4,256,128]{4,3,2,1,0:T(8,128)} %gap_hbm.1), custom_call_target="tpu_custom_call" | custom-call | tf_op jit(solution)/shard_map/feti_chebyshev/pallas_call | solution.py:323
  46.6 1.9 %copy.9 = f32[1,1,4,256,128]{4,3,2,1,0:T(8,128)} copy(f32[1,1,4,256,128]{4,3,2,1,0:T(8,128)} %get-tuple-element.4) | data formatting | bytes 1048576
  48.5 1.9 %copy.10 = f32[1,1,4,256,128]{4,3,2,1,0:T(8,128)} copy(f32[1,1,4,256,128]{4,3,2,1,0:T(8,128)} %get-tuple-element.5) | data formatting | bytes 1048576
where the time goes:
time: 50.6 us; the launch traced here: 50.4 us
  Pallas kernels  45.4 us (90%)
  local copies, waits for them, and re-layouts  3.74 us (7%)
  between operations  1.28 us (3%)
    pallas_call x1, Pallas kernels, shards(): pl.pallas_call(functools.partial(kernel, far), out_shape=(block, block),...  45.4 us
    unnamed x2, local copies, waits for them, and re-layouts  3.74 us

commit v1 on v0

v1 whole, which is shorter than its diff:
```python
import functools

import jax
import jax.numpy as jnp
from jax import lax
from jax.experimental import pallas as pl
from jax.experimental.pallas import tpu as pltpu
from jax.sharding import PartitionSpec as P

M = 512
H = 256
RHS = 128
SLOTS = 4
ITERS = 6
CHUNKS = 2
W = RHS // CHUNKS

LOWER = 1.0
UPPER = 14.0
CENTRE = (UPPER + LOWER) / 2.0
RADIUS = (UPPER - LOWER) / 2.0

F32 = jnp.float32
BF16 = jnp.bfloat16


def coefficients():
    spread = CENTRE / RADIUS
    rho = 1.0 / spread
    keep, add = {1: 0.0}, {1: 1.0 / CENTRE}
    for t in range(2, ITERS + 1):
        new = 1.0 / (2.0 * spread - rho)
        keep[t] = new * rho
        add[t] = 2.0 * new / RADIUS
        rho = new
    return keep, add


KEEP, ADD = coefficients()


def chosen(table, t):
    value = jnp.float32(table[ITERS])
    for k in range(1, ITERS):
        value = jnp.where(t == k, jnp.float32(table[k]), value)
    return value


def halves(x):
    high = x.astype(BF16)
    low = (x - high.astype(F32)).astype(BF16)
    return high, low


def nn(a, b):
    return jnp.dot(a, b, preferred_element_type=F32)


def nt(a, b):
    return lax.dot_general(a, b, (((1,), (1,)), ((), ())), preferred_element_type=F32)


def kernel(far, cnt_ref, pairs_ref, ops_hbm, gap, out_x, out_r,
           ops, w_in, w_p, w_ll, w_lr, w_far, vb, far_out, v_ghost, r_ghost, v_end, r_end, x_end, v_in, r_in, x_in, own,
           p_out, p_got, q_out, q_got, ll_out, ll_got,
           load_sem, ll_sem, p_send, p_recv, q_send, q_recv):
    s = lax.axis_index("sub")
    has_left = s > 0
    has_right = s < lax.axis_size("sub") - 1
    c = cnt_ref[0, 0]
    final_slot = jnp.clip(c - 1, 0, SLOTS - 1)

    loads = [pltpu.make_async_copy(ops_hbm.at[0, 0, j], ops.at[j], load_sem.at[j]) for j in range(SLOTS)]
    for load in loads:
        load.start()

    barrier = pltpu.get_barrier_semaphore()

    @pl.when(has_left)
    def _():
        pl.semaphore_signal(barrier, inc=1, device_id={"sub": s - 1}, device_id_type=pl.DeviceIdType.MESH)

    @pl.when(has_right)
    def _():
        pl.semaphore_signal(barrier, inc=1, device_id={"sub": s + 1}, device_id_type=pl.DeviceIdType.MESH)

    @pl.when(jnp.logical_not(has_left))
    def _():
        p_got[...] = jnp.zeros_like(p_got)

    @pl.when(jnp.logical_not(has_right))
    def _():
        q_got[...] = jnp.zeros_like(q_got)

    for ref in (v_ghost, r_ghost, v_end, r_end, x_end, own, x_in, far_out, w_far):
        ref[...] = jnp.zeros_like(ref)
    q_out[0] = jnp.zeros(q_out.shape[1:], F32)
    q_got[0] = jnp.zeros(q_got.shape[1:], F32)

    def p_copy(t, h):
        return pltpu.make_async_remote_copy(
            src_ref=p_out.at[t, h], dst_ref=p_got.at[t, h], send_sem=p_send.at[h], recv_sem=p_recv.at[t, h],
            device_id={"sub": s + 1}, device_id_type=pl.DeviceIdType.MESH)

    def q_copy(t, h):
        return pltpu.make_async_remote_copy(
            src_ref=q_out.at[t, h], dst_ref=q_got.at[t, h], send_sem=q_send.at[h], recv_sem=q_recv.at[t, h],
            device_id={"sub": s - 1}, device_id_type=pl.DeviceIdType.MESH)

    ll_copy = pltpu.make_async_remote_copy(
        src_ref=ll_out, dst_ref=ll_got, send_sem=ll_sem.at[0], recv_sem=ll_sem.at[1],
        device_id={"sub": s - 1}, device_id_type=pl.DeviceIdType.MESH)

    top = jnp.where(has_right, jnp.transpose(gap[0, 0, final_slot]), 0.0)
    for h in range(CHUNKS):
        p_out[0, h] = -top[h * W:(h + 1) * W]
    for j in range(SLOTS - 1):
        turned_gap = jnp.where(j < c - 1, jnp.transpose(gap[0, 0, j]), 0.0)
        for h in range(CHUNKS):
            r = turned_gap[h * W:(h + 1) * W]
            r_in[h, j] = r
            v_in[h, j] = r * (1.0 / CENTRE)

    rows = lax.broadcasted_iota(jnp.int32, (H, H), 0)

    def selection(pairs):
        sign = jnp.where(pairs > 0, -1.0, 1.0)
        return jnp.where(rows == jnp.abs(pairs) - 1, sign, 0.0).astype(BF16)

    def turned(picked, block):
        high, low = halves(block)
        return nt(picked, high).astype(BF16), nt(picked, low).astype(BF16)

    def left_left(picked, j):
        high, low = turned(picked, ops[j, :H, :H])
        return nt(high, picked), nt(low, picked)

    def left_right(picked, j):
        high, low = halves(jnp.transpose(ops[j, :H, H:]))
        return nt(high, picked).astype(BF16), nt(low, picked).astype(BF16)

    pairs = [pairs_ref[0, 0, j:j + 1, :] for j in range(SLOTS)]
    loads[0].wait()
    picked = selection(pairs[0])
    ll_high, ll_low = left_left(picked, 0)
    ll_out[...] = ll_high + ll_low
    w_ll[0] = ll_high.astype(BF16)
    w_ll[1] = ll_low.astype(BF16)
    w_lr[0], w_lr[1] = left_right(picked, 0)

    for load in loads[1:]:
        load.wait()
    last_pairs = jnp.where(c == 1, pairs[0], jnp.where(c == 2, pairs[1], jnp.where(c == 3, pairs[2], pairs[3])))
    w_p[0, :H], w_p[1, :H] = turned(selection(last_pairs), ops[final_slot, H:, :H])
    w_p[0, H:], w_p[1, H:] = halves(jnp.transpose(ops[final_slot, H:, H:]))

    pl.semaphore_wait(barrier, has_left.astype(jnp.int32) + has_right.astype(jnp.int32))

    @pl.when(has_right)
    def _():
        for h in range(CHUNKS):
            p_copy(0, h).start()

    @pl.when(has_left)
    def _():
        ll_copy.start()

    def product(x, w):
        high, low = x
        both = nn(jnp.concatenate([high, low], axis=0), w[0])
        return (both[:W] + both[W:]) + nn(high, w[1])

    def end_step(t, h, last):
        keep, add = chosen(KEEP, t), chosen(ADD, t)
        partial = p_out[t - 1, h] + far_out[h]

        @pl.when(jnp.logical_and(has_right, t > 1))
        def _():
            q_copy(t - 1, h).wait_recv()

        r = r_end[h] - jnp.where(has_right, partial + q_got[t - 1, h], 0.0)
        r_end[h] = r

        def rest():
            end = keep * v_end[h] + add * r
            q_out[t, h] = product(halves(jnp.where(c == 1, end, v_in[h, 0])), w_lr)

            @pl.when(has_left)
            def _():
                @pl.when(t > 1)
                def _():
                    q_copy(t - 1, h).wait_send()

                q_copy(t, h).start()

            v_end[h] = end
            x_end[h] = x_end[h] + end
            far_out[h] = product(halves(end), w_far)

        if last:
            pl.when(t <= ITERS)(rest)
        else:
            rest()

    def late_far():
        @pl.when(has_right)
        def _():
            ll_copy.wait_recv()
            w_far[0], w_far[1] = halves(ll_got[...])
            for h in range(CHUNKS):
                far_out[h] = product(halves(v_end[h]), w_far)

    def row(t, h, j):
        y = product((vb[h, :W, j * H:(j + 3) * H], vb[h, W:, j * H:(j + 3) * H]), w_in.at[j])
        r = r_in[h, j] - jnp.where(j < c - 1, y, 0.0)
        v = v_in[h, j]
        r_in[h, j] = r
        x_in[h, j] = x_in[h, j] + v
        v_in[h, j] = chosen(KEEP, t + 1) * v + chosen(ADD, t + 1) * r

    def ghost_step(t, h):
        keep, add = chosen(KEEP, t), chosen(ADD, t)
        partial = q_out[t - 1, h] + own[h]
        inner = [v_in[h, j] for j in range(3)]
        end = v_end[h]

        @pl.when(has_left)
        def _():
            p_copy(t - 1, h).wait_recv()

        r = r_ghost[h] - jnp.where(has_left, partial + p_got[t - 1, h], 0.0)
        ghost = keep * v_ghost[h] + add * r
        before = jnp.where(c == 1, ghost, jnp.where(c == 2, inner[0], jnp.where(c == 3, inner[1], inner[2])))
        end_high, end_low = halves(end)
        high, low = halves(before)
        p_out[t, h] = product((jnp.concatenate([high, end_high], axis=1), jnp.concatenate([low, end_low], axis=1)), w_p)

        @pl.when(has_right)
        def _():
            p_copy(t - 1, h).wait_send()

            @pl.when(t < ITERS)
            def _():
                p_copy(t, h).start()

        r_ghost[h] = r
        v_ghost[h] = ghost
        for i, block in enumerate([ghost] + [jnp.where(c == j + 1, end, inner[j]) for j in range(3)] + [end]):
            high, low = halves(block)
            vb[h, :W, i * H:(i + 1) * H] = high
            vb[h, W:, i * H:(i + 1) * H] = low
        row(t, h, 0)

    def inner_step(t, h):
        row(t, h, 1)
        row(t, h, 2)
        own[h] = product((vb[h, :W, :H], vb[h, W:, :H]), w_ll)

    left_is_far = s % far == 0

    @pl.when(left_is_far)
    def _():
        @pl.loop(0, CHUNKS)
        def _(h):
            end_step(1, h, False)

    for j in range(SLOTS):
        picked = selection(pairs[j])
        if j > 0:
            ll_high, ll_low = left_left(picked, j)
            mid_high, mid_low = halves(jnp.transpose(ops[j - 1, H:, H:]) + (ll_high + ll_low))
            w_in[j - 1, 0, H:2 * H] = mid_high
            w_in[j - 1, 1, H:2 * H] = mid_low
            w_in[j - 1, 0, 2 * H:], w_in[j - 1, 1, 2 * H:] = left_right(picked, j)
        if j < SLOTS - 1:
            w_in[j, 0, :H], w_in[j, 1, :H] = turned(picked, ops[j, H:, :H])

    def placed(inner, end, j):
        kept = jnp.where(j < c - 1, inner, 0.0) if j < 3 else jnp.zeros_like(end)
        return jnp.transpose(jnp.where(c - 1 == j, end, kept))

    @pl.when(left_is_far)
    def _():
        late_far()

        @pl.loop(0, ITERS * CHUNKS)
        def _(n):
            t, h = n // CHUNKS + 1, n % CHUNKS
            ghost_step(t, h)
            end_step(t + 1, h, True)
            inner_step(t, h)

    @pl.when(jnp.logical_not(left_is_far))
    def _():
        @pl.loop(0, ITERS * CHUNKS)
        def _(n):
            t, h = n // CHUNKS + 1, n % CHUNKS
            end_step(t, h, False)
            ghost_step(t, h)
            inner_step(t, h)
            pl.when(n == CHUNKS - 1)(late_far)

    end = x_end[...].reshape(RHS, H)
    for j in range(SLOTS):
        out_x[0, 0, j] = placed(x_in[:, j % 3].reshape(RHS, H), end, j)
        out_r[0, 0, j] = placed(r_in[:, j % 3].reshape(RHS, H), jnp.zeros_like(end), j)

    @pl.when(jnp.logical_and(jnp.logical_not(left_is_far), has_right))
    def _():
        @pl.loop(0, CHUNKS)
        def _(h):
            q_copy(ITERS, h).wait_recv()
            r_end[h] = r_end[h] - (p_out[ITERS, h] + far_out[h] + q_got[ITERS, h])

    end = jnp.transpose(r_end[...].reshape(RHS, H))
    for j in range(SLOTS):
        out_r[0, 0, j] = jnp.where(c - 1 == j, end, out_r[0, 0, j])

    @pl.when(has_left)
    def _():
        ll_copy.wait_send()
        for h in range(CHUNKS):
            q_copy(ITERS, h).wait_send()


def shards(far, operators, counts, pair_rows, gap):
    hbm = pl.BlockSpec(memory_space=pltpu.HBM)
    vmem = pl.BlockSpec(memory_space=pltpu.VMEM)
    dma = pltpu.SemaphoreType.DMA
    message = pltpu.VMEM((ITERS + 1, CHUNKS, W, H), F32)
    chunk = pltpu.VMEM((CHUNKS, W, H), F32)
    inner = pltpu.VMEM((CHUNKS, 3, W, H), F32)
    operator = pltpu.VMEM((2, H, H), BF16)
    block = jax.ShapeDtypeStruct((1, 1, SLOTS, H, RHS), F32)
    return pl.pallas_call(
        functools.partial(kernel, far),
        out_shape=(block, block),
        in_specs=[pl.BlockSpec(memory_space=pltpu.SMEM), vmem, hbm, vmem],
        out_specs=(vmem, vmem),
        scratch_shapes=[
            pltpu.VMEM((SLOTS, M, M), F32),
            pltpu.VMEM((3, 2, 3 * H, H), BF16),
            pltpu.VMEM((2, 2 * H, H), BF16),
            operator,
            operator,
            operator,
            pltpu.VMEM((CHUNKS, 2 * W, 5 * H), BF16),
            chunk, chunk, chunk, chunk, chunk, chunk,
            inner, inner, inner,
            chunk,
            message, message, message, message,
            pltpu.VMEM((H, H), F32),
            pltpu.VMEM((H, H), F32),
            dma((SLOTS,)),
            dma((2,)),
            dma((CHUNKS,)),
            dma((ITERS + 1, CHUNKS)),
            dma((CHUNKS,)),
            dma((ITERS + 1, CHUNKS)),
        ],
        compiler_params=pltpu.CompilerParams(
            collective_id=0, has_side_effects=True, vmem_limit_bytes=54_000_000),
        name="feti_chebyshev",
    )(counts, pair_rows, operators, gap)


def solution(mesh):
    return jax.shard_map(
        functools.partial(shards, 16 if mesh.shape["sub"] % 16 == 0 else 2),
        mesh=mesh,
        in_specs=(
            P("grp", "sub", None, None, None),
            P("grp", "sub"),
            P("grp", "sub", None, None),
            P("grp", "sub", None, None, None),
        ),
        out_specs=(P("grp", "sub", None, None, None), P("grp", "sub", None, None, None)),
        check_vma=False,
    )
```

time: 50.6 us -> 49.1 us (0.970)
  Pallas kernels: 45.4 us -> 44.3 us
    pallas_call x1, Pallas kernels: 45.4 us -> 44.3 us  [shards(): pl.pallas_call(functools.partial(kernel, far), out_shape=(block, block),...]
    unnamed x2 -> x6, local copies, waits for them, and re-layouts: 3.74 us -> 3.31 us
where the time goes in v1:
time: 49.1 us; the launch traced here: 48.9 us
  Pallas kernels  44.3 us (90%)
  local copies, waits for them, and re-layouts  3.31 us (7%)
  between operations  1.29 us (3%)
    pallas_call x1, Pallas kernels, shards(): pl.pallas_call(functools.partial(kernel, far), out_shape=(block, block),...  44.3 us
    unnamed x6, local copies, waits for them, and re-layouts  3.31 us

profile of v1, /device:TPU:24, one launch (start us, length us, event | category | flops | bytes accessed | tf_op | source)
XLA Modules:
  0.0 48.9 jit_solution(7831516620799828269)
XLA Ops:
  1.3 0.0 copy-start
  1.3 1.0 %copy-done = f32[1,1,4,256,128]{4,3,2,1,0:T(8,128)S(1)} copy-done((f32[1,1,4,256,128]{4,3,2,1,0:T(8,128)S(1)}, f32[1,1,4,256,128]{4,3,2,1,0:T(8,128)}, u32[]{:S(2)}) %copy-start) | copy-done | bytes 524312
  2.3 0.0 copy-start.1
  2.3 0.7 %copy-done.1 = s32[1,1,4,256]{3,2,1,0:T(4,128)S(1)} copy-done((s32[1,1,4,256]{3,2,1,0:T(4,128)S(1)}, s32[1,1,4,256]{3,2,1,0:T(4,128)}, u32[]{:S(2)}) %copy-start.1) | copy-done | bytes 4120
  3.0 44.3 %feti_chebyshev.1 = (f32[1,1,4,256,128]{4,3,2,1,0:T(8,128)S(1)}, f32[1,1,4,256,128]{4,3,2,1,0:T(8,128)S(1)}) custom-call(s32[1,1]{1,0:T(1,128)S(6)} %copy.8.cnt_ref, s32[1,1,4,256]{3,2,1,0:T(4,128)S(1)} %copy-done.1, f32[1,1,4,512,512]{4,3,2,1,0:T(8,128)} %ops_hbm.1, f32[1,1,4,256,128]{4,3,2,1,0:T(8,128)S(1)} %copy-done), custom_call_target="tpu_custom_call" | custom-call | tf_op jit(solution)/shard_map/feti_chebyshev/pallas_call | solution.py:335
  47.3 0.8 %copy.9 = f32[1,1,4,256,128]{4,3,2,1,0:T(8,128)} copy(f32[1,1,4,256,128]{4,3,2,1,0:T(8,128)S(1)} %get-tuple-element.4) | data formatting | bytes 1048576
  48.1 0.8 %copy.10 = f32[1,1,4,256,128]{4,3,2,1,0:T(8,128)} copy(f32[1,1,4,256,128]{4,3,2,1,0:T(8,128)S(1)} %get-tuple-element.5) | data formatting | bytes 1048576
Async XLA Ops:
  1.3 1.0 %copy-start = (f32[1,1,4,256,128]{4,3,2,1,0:T(8,128)S(1)}, f32[1,1,4,256,128]{4,3,2,1,0:T(8,128)}, u32[]{:S(2)}) copy-start(f32[1,1,4,256,128]{4,3,2,1,0:T(8,128)} %gap.1) | copy-start | bytes 1572868
  2.3 0.7 %copy-start.1 = (s32[1,1,4,256]{3,2,1,0:T(4,128)S(1)}, s32[1,1,4,256]{3,2,1,0:T(4,128)}, u32[]{:S(2)}) copy-start(s32[1,1,4,256]{3,2,1,0:T(4,128)} %pairs_ref.1) | copy-start | bytes 12292

commit v2 on v1

--- a/solution.py
+++ b/solution.py
@@ -33,6 +33,7 @@
         keep[t] = new * rho
         add[t] = 2.0 * new / RADIUS
         rho = new
+    keep[ITERS + 1] = add[ITERS + 1] = 0.0
     return keep, add
 
 
@@ -40,8 +41,8 @@
 
 
 def chosen(table, t):
-    value = jnp.float32(table[ITERS])
-    for k in range(1, ITERS):
+    value = jnp.float32(table[ITERS + 1])
+    for k in range(1, ITERS + 1):
         value = jnp.where(t == k, jnp.float32(table[k]), value)
     return value
 
@@ -60,30 +61,34 @@
     return lax.dot_general(a, b, (((1,), (1,)), ((), ())), preferred_element_type=F32)
 
 
-def kernel(far, cnt_ref, pairs_ref, ops_hbm, gap, out_x, out_r,
-           ops, w_in, w_p, w_ll, w_lr, w_far, vb, far_out, v_ghost, r_ghost, v_end, r_end, x_end, v_in, r_in, x_in, own,
+def kernel(far, cnt_ref, pairs_hbm, ops_hbm, gap_hbm, out_x, out_r,
+           ops, gap, pairs_ref, w_in, w_p, w_ll, w_lr, w_far, vb, far_out, v_ghost, r_ghost, v_end, r_end, x_end, v_in, r_in, x_in, own,
            p_out, p_got, q_out, q_got, ll_out, ll_got,
-           load_sem, ll_sem, p_send, p_recv, q_send, q_recv):
+           load_sem, gap_sem, ll_sem, p_send, p_recv, q_send, q_recv):
     s = lax.axis_index("sub")
     has_left = s > 0
     has_right = s < lax.axis_size("sub") - 1
     c = cnt_ref[0, 0]
     final_slot = jnp.clip(c - 1, 0, SLOTS - 1)
 
+    barrier = pltpu.get_barrier_semaphore()
+
+    @pl.when(has_left)
+    def _():
+        pl.semaphore_signal(barrier, inc=1, device_id={"sub": s - 1}, device_id_type=pl.DeviceIdType.MESH)
+
+    @pl.when(has_right)
+    def _():
+        pl.semaphore_signal(barrier, inc=1, device_id={"sub": s + 1}, device_id_type=pl.DeviceIdType.MESH)
+
+    pairs_load = pltpu.make_async_copy(pairs_hbm.at[0, 0], pairs_ref, gap_sem.at[1])
+    pairs_load.start()
+    gap_load = pltpu.make_async_copy(gap_hbm.at[0, 0], gap, gap_sem.at[0])
+    gap_load.start()
     loads = [pltpu.make_async_copy(ops_hbm.at[0, 0, j], ops.at[j], load_sem.at[j]) for j in range(SLOTS)]
     for load in loads:
         load.start()
 
-    barrier = pltpu.get_barrier_semaphore()
-
-    @pl.when(has_left)
-    def _():
-        pl.semaphore_signal(barrier, inc=1, device_id={"sub": s - 1}, device_id_type=pl.DeviceIdType.MESH)
-
-    @pl.when(has_right)
-    def _():
-        pl.semaphore_signal(barrier, inc=1, device_id={"sub": s + 1}, device_id_type=pl.DeviceIdType.MESH)
-
     @pl.when(jnp.logical_not(has_left))
     def _():
         p_got[...] = jnp.zeros_like(p_got)
@@ -92,7 +97,7 @@
     def _():
         q_got[...] = jnp.zeros_like(q_got)
 
-    for ref in (v_ghost, r_ghost, v_end, r_end, x_end, own, x_in, far_out, w_far):
+    for ref in (v_ghost, r_ghost, v_end, r_end, x_end, own, far_out, w_far):
         ref[...] = jnp.zeros_like(ref)
     q_out[0] = jnp.zeros(q_out.shape[1:], F32)
     q_got[0] = jnp.zeros(q_got.shape[1:], F32)
@@ -111,15 +116,17 @@
         src_ref=ll_out, dst_ref=ll_got, send_sem=ll_sem.at[0], recv_sem=ll_sem.at[1],
         device_id={"sub": s - 1}, device_id_type=pl.DeviceIdType.MESH)
 
-    top = jnp.where(has_right, jnp.transpose(gap[0, 0, final_slot]), 0.0)
+    gap_load.wait()
+    top = jnp.where(has_right, jnp.transpose(gap[final_slot]), 0.0)
     for h in range(CHUNKS):
         p_out[0, h] = -top[h * W:(h + 1) * W]
     for j in range(SLOTS - 1):
-        turned_gap = jnp.where(j < c - 1, jnp.transpose(gap[0, 0, j]), 0.0)
+        turned_gap = jnp.where(j < c - 1, jnp.transpose(gap[j]), 0.0)
         for h in range(CHUNKS):
             r = turned_gap[h * W:(h + 1) * W]
             r_in[h, j] = r
             v_in[h, j] = r * (1.0 / CENTRE)
+            x_in[h, j] = r * (1.0 / CENTRE)
 
     rows = lax.broadcasted_iota(jnp.int32, (H, H), 0)
 
@@ -139,7 +146,8 @@
         high, low = halves(jnp.transpose(ops[j, :H, H:]))
         return nt(high, picked).astype(BF16), nt(low, picked).astype(BF16)
 
-    pairs = [pairs_ref[0, 0, j:j + 1, :] for j in range(SLOTS)]
+    pairs_load.wait()
+    pairs = [pairs_ref[j:j + 1, :] for j in range(SLOTS)]
     loads[0].wait()
     picked = selection(pairs[0])
     ll_high, ll_low = left_left(picked, 0)
@@ -161,7 +169,9 @@
         for h in range(CHUNKS):
             p_copy(0, h).start()
 
-    @pl.when(has_left)
+    goes_first = lax.axis_index("grp") % 2 == 0
+
+    @pl.when(jnp.logical_and(has_left, goes_first))
     def _():
         ll_copy.start()
 
@@ -214,9 +224,10 @@
         y = product((vb[h, :W, j * H:(j + 3) * H], vb[h, W:, j * H:(j + 3) * H]), w_in.at[j])
         r = r_in[h, j] - jnp.where(j < c - 1, y, 0.0)
         v = v_in[h, j]
+        v = chosen(KEEP, t + 1) * v + chosen(ADD, t + 1) * r
         r_in[h, j] = r
+        v_in[h, j] = v
         x_in[h, j] = x_in[h, j] + v
-        v_in[h, j] = chosen(KEEP, t + 1) * v + chosen(ADD, t + 1) * r
 
     def ghost_step(t, h):
         keep, add = chosen(KEEP, t), chosen(ADD, t)
@@ -275,10 +286,19 @@
         if j < SLOTS - 1:
             w_in[j, 0, :H], w_in[j, 1, :H] = turned(picked, ops[j, H:, :H])
 
+    @pl.when(jnp.logical_and(has_left, jnp.logical_not(goes_first)))
+    def _():
+        ll_copy.start()
+
     def placed(inner, end, j):
         kept = jnp.where(j < c - 1, inner, 0.0) if j < 3 else jnp.zeros_like(end)
         return jnp.transpose(jnp.where(c - 1 == j, end, kept))
 
+    def finish_x():
+        end = x_end[...].reshape(RHS, H)
+        for j in range(SLOTS):
+            out_x[0, 0, j] = placed(x_in[:, j % 3].reshape(RHS, H), end, j)
+
     @pl.when(left_is_far)
     def _():
         late_far()
@@ -286,6 +306,7 @@
         @pl.loop(0, ITERS * CHUNKS)
         def _(n):
             t, h = n // CHUNKS + 1, n % CHUNKS
+            pl.when(n == ITERS * CHUNKS - 1)(finish_x)
             ghost_step(t, h)
             end_step(t + 1, h, True)
             inner_step(t, h)
@@ -296,14 +317,14 @@
         def _(n):
             t, h = n // CHUNKS + 1, n % CHUNKS
             end_step(t, h, False)
+            pl.when(n == ITERS * CHUNKS - 1)(finish_x)
             ghost_step(t, h)
             inner_step(t, h)
             pl.when(n == CHUNKS - 1)(late_far)
 
-    end = x_end[...].reshape(RHS, H)
+    end = jnp.zeros((RHS, H), F32)
     for j in range(SLOTS):
-        out_x[0, 0, j] = placed(x_in[:, j % 3].reshape(RHS, H), end, j)
-        out_r[0, 0, j] = placed(r_in[:, j % 3].reshape(RHS, H), jnp.zeros_like(end), j)
+        out_r[0, 0, j] = placed(r_in[:, j % 3].reshape(RHS, H), end, j)
 
     @pl.when(jnp.logical_and(jnp.logical_not(left_is_far), has_right))
     def _():
@@ -321,6 +342,14 @@
         ll_copy.wait_send()
         for h in range(CHUNKS):
             q_copy(ITERS, h).wait_send()
+
+
+def put_out(x, r, out_x, out_r, sems):
+    stores = [pltpu.make_async_copy(x, out_x, sems.at[0]), pltpu.make_async_copy(r, out_r, sems.at[1])]
+    for store in stores:
+        store.start()
+    for store in stores:
+        store.wait()
 
 
 def shards(far, operators, counts, pair_rows, gap):
@@ -332,13 +361,15 @@
     inner = pltpu.VMEM((CHUNKS, 3, W, H), F32)
     operator = pltpu.VMEM((2, H, H), BF16)
     block = jax.ShapeDtypeStruct((1, 1, SLOTS, H, RHS), F32)
-    return pl.pallas_call(
+    results = pl.pallas_call(
         functools.partial(kernel, far),
         out_shape=(block, block),
-        in_specs=[pl.BlockSpec(memory_space=pltpu.SMEM), vmem, hbm, vmem],
+        in_specs=[pl.BlockSpec(memory_space=pltpu.SMEM), hbm, hbm, hbm],
         out_specs=(vmem, vmem),
         scratch_shapes=[
             pltpu.VMEM((SLOTS, M, M), F32),
+            pltpu.VMEM((SLOTS, H, RHS), F32),
+            pltpu.VMEM((SLOTS, H), jnp.int32),
             pltpu.VMEM((3, 2, 3 * H, H), BF16),
             pltpu.VMEM((2, 2 * H, H), BF16),
             operator,
@@ -353,15 +384,25 @@
             pltpu.VMEM((H, H), F32),
             dma((SLOTS,)),
             dma((2,)),
+            dma((2,)),
             dma((CHUNKS,)),
             dma((ITERS + 1, CHUNKS)),
             dma((CHUNKS,)),
             dma((ITERS + 1, CHUNKS)),
         ],
         compiler_params=pltpu.CompilerParams(
-            collective_id=0, has_side_effects=True, vmem_limit_bytes=54_000_000),
+            collective_id=0, has_side_effects=True, vmem_limit_bytes=55_200_000),
         name="feti_chebyshev",
     )(counts, pair_rows, operators, gap)
+    return pl.pallas_call(
+        put_out,
+        out_shape=(block, block),
+        in_specs=[vmem, vmem],
+        out_specs=(hbm, hbm),
+        scratch_shapes=[dma((2,))],
+        compiler_params=pltpu.CompilerParams(vmem_limit_bytes=8 * 1024 * 1024),
+        name="put_out",
+    )(*results)
 
 
 def solution(mesh):

time: 49.1 us -> 46.7 us (0.951)
  local copies, waits for them, and re-layouts: 3.31 us -> 0.68 us
    unnamed x6 -> x2, local copies, waits for them, and re-layouts: 3.31 us -> 0.68 us
    pallas_call x0 -> x1, Pallas kernels: none -> 0.99 us  [shards(): pl.pallas_call(put_out, out_shape=(block, block), in_specs=[vmem, vmem],...]
    pallas_call x1, Pallas kernels: 44.3 us -> 43.6 us  [shards(): pl.pallas_call(functools.partial(kernel, far), out_shape=(block, block),...]
where the time goes in v2:
time: 46.7 us; the launch traced here: 46.6 us
  Pallas kernels  44.6 us (96%)
  between operations  1.29 us (3%)
  local copies, waits for them, and re-layouts  0.68 us (1%)
    pallas_call x1, Pallas kernels, shards(): pl.pallas_call(functools.partial(kernel, far), out_shape=(block, block),...  43.6 us
    pallas_call x1, Pallas kernels, shards(): pl.pallas_call(put_out, out_shape=(block, block), in_specs=[vmem, vmem],...  0.99 us

profile of v2, /device:TPU:24, one launch (start us, length us, event | category | flops | bytes accessed | tf_op | source)
XLA Modules:
  0.0 46.6 jit_solution(6333978635765139956)
XLA Ops:
  1.3 0.0 copy-start
  1.3 0.7 %copy-done = s32[1,1,4,256]{3,2,1,0:T(4,128)S(1)} copy-done((s32[1,1,4,256]{3,2,1,0:T(4,128)S(1)}, s32[1,1,4,256]{3,2,1,0:T(4,128)}, u32[]{:S(2)}) %copy-start) | copy-done | bytes 4120
  2.0 43.6 %feti_chebyshev.1 = (f32[1,1,4,256,128]{4,3,2,1,0:T(8,128)S(1)}, f32[1,1,4,256,128]{4,3,2,1,0:T(8,128)S(1)}) custom-call(s32[1,1]{1,0:T(1,128)S(6)} %copy.6.cnt_ref, s32[1,1,4,256]{3,2,1,0:T(4,128)S(1)} %copy-done, f32[1,1,4,512,512]{4,3,2,1,0:T(8,128)} %ops_hbm.1, f32[1,1,4,256,128]{4,3,2,1,0:T(8,128)} %gap_hbm.1), custom_call_target="tpu_custom_call" | custom-call | tf_op jit(solution)/shard_map/feti_chebyshev/pallas_call | solution.py:364
  45.6 1.0 %put_out.1 = (f32[1,1,4,256,128]{4,3,2,1,0:T(8,128)}, f32[1,1,4,256,128]{4,3,2,1,0:T(8,128)}) custom-call(f32[1,1,4,256,128]{4,3,2,1,0:T(8,128)S(1)} %get-tuple-element.4.x, f32[1,1,4,256,128]{4,3,2,1,0:T(8,128)S(1)} %get-tuple-element.5.r), custom_call_target="tpu_custom_call" | custom-call | tf_op jit(solution)/shard_map/put_out/pallas_call | solution.py:397
Async XLA Ops:
  1.3 0.7 %copy-start = (s32[1,1,4,256]{3,2,1,0:T(4,128)S(1)}, s32[1,1,4,256]{3,2,1,0:T(4,128)}, u32[]{:S(2)}) copy-start(s32[1,1,4,256]{3,2,1,0:T(4,128)} %pairs_hbm.1) | copy-start | bytes 12292

commit v3 on v2

--- a/solution.py
+++ b/solution.py
@@ -62,12 +62,15 @@
 
 
 def kernel(far, cnt_ref, pairs_hbm, ops_hbm, gap_hbm, out_x, out_r,
-           ops, gap, pairs_ref, w_in, w_p, w_ll, w_lr, w_far, vb, far_out, v_ghost, r_ghost, v_end, r_end, x_end, v_in, r_in, x_in, own,
+           ops, gap, pairs_ref, w_in, w_p, w_ll, w_lr, w_far, vb, far_out, pg_out, pl_out, row_out, before_in, v_ghost, r_ghost, v_end, r_end, x_end, v_in, r_in, x_in, own,
            p_out, p_got, q_out, q_got, ll_out, ll_got,
            load_sem, gap_sem, ll_sem, p_send, p_recv, q_send, q_recv):
     s = lax.axis_index("sub")
     has_left = s > 0
     has_right = s < lax.axis_size("sub") - 1
+    left_is_far = s % far == 0
+    right_is_far = s % far == far - 1
+    both_near = jnp.logical_not(jnp.logical_or(left_is_far, right_is_far))
     c = cnt_ref[0, 0]
     final_slot = jnp.clip(c - 1, 0, SLOTS - 1)
 
@@ -120,6 +123,17 @@
     top = jnp.where(has_right, jnp.transpose(gap[final_slot]), 0.0)
     for h in range(CHUNKS):
         p_out[0, h] = -top[h * W:(h + 1) * W]
+
+    def open_gate():
+        pl.semaphore_wait(barrier, has_left.astype(jnp.int32) + has_right.astype(jnp.int32))
+
+        @pl.when(has_right)
+        def _():
+            for h in range(CHUNKS):
+                p_copy(0, h).start()
+
+    pl.when(both_near)(open_gate)
+
     for j in range(SLOTS - 1):
         turned_gap = jnp.where(j < c - 1, jnp.transpose(gap[j]), 0.0)
         for h in range(CHUNKS):
@@ -162,12 +176,7 @@
     w_p[0, :H], w_p[1, :H] = turned(selection(last_pairs), ops[final_slot, H:, :H])
     w_p[0, H:], w_p[1, H:] = halves(jnp.transpose(ops[final_slot, H:, H:]))
 
-    pl.semaphore_wait(barrier, has_left.astype(jnp.int32) + has_right.astype(jnp.int32))
-
-    @pl.when(has_right)
-    def _():
-        for h in range(CHUNKS):
-            p_copy(0, h).start()
+    pl.when(jnp.logical_not(both_near))(open_gate)
 
     goes_first = lax.axis_index("grp") % 2 == 0
 
@@ -176,13 +185,22 @@
         ll_copy.start()
 
     def product(x, w):
-        high, low = x
-        both = nn(jnp.concatenate([high, low], axis=0), w[0])
-        return (both[:W] + both[W:]) + nn(high, w[1])
-
-    def end_step(t, h, last):
+        both = nn(jnp.concatenate(x, axis=0), w[0])
+        return (both[:W] + both[W:]) + nn(x[0], w[1])
+
+    def send_p(t, h):
+        @pl.when(has_right)
+        def _():
+            p_copy(t - 1, h).wait_send()
+
+            @pl.when(t < ITERS)
+            def _():
+                p_copy(t, h).start()
+
+    def end_part(t, h, sends_p=False, guarded=False):
         keep, add = chosen(KEEP, t), chosen(ADD, t)
         partial = p_out[t - 1, h] + far_out[h]
+        first = v_in[h, 0]
 
         @pl.when(jnp.logical_and(has_right, t > 1))
         def _():
@@ -193,7 +211,11 @@
 
         def rest():
             end = keep * v_end[h] + add * r
-            q_out[t, h] = product(halves(jnp.where(c == 1, end, v_in[h, 0])), w_lr)
+            split = halves(end)
+            if sends_p:
+                p_out[t, h] = pg_out[h] + product(split, (w_p[0, H:], w_p[1, H:]))
+                send_p(t, h)
+            q_out[t, h] = product(halves(jnp.where(c == 1, end, first)), w_lr)
 
             @pl.when(has_left)
             def _():
@@ -203,11 +225,15 @@
 
                 q_copy(t, h).start()
 
+            if not sends_p:
+                pl_out[h] = product(split, (w_p[0, H:], w_p[1, H:]))
             v_end[h] = end
             x_end[h] = x_end[h] + end
-            far_out[h] = product(halves(end), w_far)
-
-        if last:
+            far_out[h] = product(split, w_far)
+            if guarded:
+                heavy_part(t, h, False)
+
+        if guarded:
             pl.when(t <= ITERS)(rest)
         else:
             rest()
@@ -220,20 +246,20 @@
             for h in range(CHUNKS):
                 far_out[h] = product(halves(v_end[h]), w_far)
 
-    def row(t, h, j):
-        y = product((vb[h, :W, j * H:(j + 3) * H], vb[h, W:, j * H:(j + 3) * H]), w_in.at[j])
+    def advance(t, h, j, y):
         r = r_in[h, j] - jnp.where(j < c - 1, y, 0.0)
-        v = v_in[h, j]
-        v = chosen(KEEP, t + 1) * v + chosen(ADD, t + 1) * r
+        v = chosen(KEEP, t + 1) * v_in[h, j] + chosen(ADD, t + 1) * r
         r_in[h, j] = r
         v_in[h, j] = v
         x_in[h, j] = x_in[h, j] + v
 
-    def ghost_step(t, h):
+    def ghost_part(t, h, sends_p=True, held=False):
         keep, add = chosen(KEEP, t), chosen(ADD, t)
         partial = q_out[t - 1, h] + own[h]
-        inner = [v_in[h, j] for j in range(3)]
-        end = v_end[h]
+        if held:
+            before = before_in[h]
+        else:
+            before = jnp.where(c == 2, v_in[h, 0], jnp.where(c == 3, v_in[h, 1], v_in[h, 2]))
 
         @pl.when(has_left)
         def _():
@@ -241,39 +267,51 @@
 
         r = r_ghost[h] - jnp.where(has_left, partial + p_got[t - 1, h], 0.0)
         ghost = keep * v_ghost[h] + add * r
-        before = jnp.where(c == 1, ghost, jnp.where(c == 2, inner[0], jnp.where(c == 3, inner[1], inner[2])))
-        end_high, end_low = halves(end)
-        high, low = halves(before)
-        p_out[t, h] = product((jnp.concatenate([high, end_high], axis=1), jnp.concatenate([low, end_low], axis=1)), w_p)
-
-        @pl.when(has_right)
-        def _():
-            p_copy(t - 1, h).wait_send()
-
-            @pl.when(t < ITERS)
-            def _():
-                p_copy(t, h).start()
-
+        split = halves(ghost)
+        from_left = product(halves(jnp.where(c == 1, ghost, before)), (w_p[0, :H], w_p[1, :H]))
+        if sends_p:
+            p_out[t, h] = from_left + pl_out[h]
+        else:
+            pg_out[h] = from_left
+        y = product(split, (w_in[0, 0, :H], w_in[0, 1, :H]))
+        if held:
+            advance(t, h, 0, y + row_out[h])
+        else:
+            row_out[h] = y
         r_ghost[h] = r
         v_ghost[h] = ghost
-        for i, block in enumerate([ghost] + [jnp.where(c == j + 1, end, inner[j]) for j in range(3)] + [end]):
-            high, low = halves(block)
-            vb[h, :W, i * H:(i + 1) * H] = high
-            vb[h, W:, i * H:(i + 1) * H] = low
-        row(t, h, 0)
-
-    def inner_step(t, h):
-        row(t, h, 1)
-        row(t, h, 2)
-        own[h] = product((vb[h, :W, :H], vb[h, W:, :H]), w_ll)
-
-    left_is_far = s % far == 0
+        if sends_p:
+            send_p(t, h)
+        own[h] = product(split, w_ll)
+
+    def heavy_part(t, h, finishes):
+        inner = [v_in[h, j] for j in range(3)]
+        end = v_end[h]
+        if not finishes:
+            before_in[h] = jnp.where(c == 2, inner[0], jnp.where(c == 3, inner[1], inner[2]))
+        blocks = [inner[0]] + [jnp.where(c == j + 1, end, inner[j]) for j in (1, 2)] + [end]
+        for i, block in enumerate(blocks):
+            high, low = halves(jnp.where(c == 1, end, block) if i == 0 else block)
+            vb[h, 0, :, i * H:(i + 1) * H] = high
+            vb[h, 1, :, i * H:(i + 1) * H] = low
+
+        def columns(k, width):
+            return vb[h, 0, :, k * H:(k + width) * H], vb[h, 1, :, k * H:(k + width) * H]
+
+        y = product(columns(0, 2), (w_in[0, 0, H:], w_in[0, 1, H:]))
+        if finishes:
+            advance(t, h, 0, y + row_out[h])
+        else:
+            row_out[h] = y
+        for j in (1, 2):
+            advance(t, h, j, product(columns(j - 1, 3), w_in.at[j]))
+
 
     @pl.when(left_is_far)
     def _():
         @pl.loop(0, CHUNKS)
         def _(h):
-            end_step(1, h, False)
+            end_part(1, h)
 
     for j in range(SLOTS):
         picked = selection(pairs[j])
@@ -299,27 +337,45 @@
         for j in range(SLOTS):
             out_x[0, 0, j] = placed(x_in[:, j % 3].reshape(RHS, H), end, j)
 
-    @pl.when(left_is_far)
-    def _():
-        late_far()
-
+    def all_steps(body):
         @pl.loop(0, ITERS * CHUNKS)
         def _(n):
-            t, h = n // CHUNKS + 1, n % CHUNKS
-            pl.when(n == ITERS * CHUNKS - 1)(finish_x)
-            ghost_step(t, h)
-            end_step(t + 1, h, True)
-            inner_step(t, h)
-
-    @pl.when(jnp.logical_not(left_is_far))
-    def _():
-        @pl.loop(0, ITERS * CHUNKS)
-        def _(n):
-            t, h = n // CHUNKS + 1, n % CHUNKS
-            end_step(t, h, False)
-            pl.when(n == ITERS * CHUNKS - 1)(finish_x)
-            ghost_step(t, h)
-            inner_step(t, h)
+            body(n // CHUNKS + 1, n % CHUNKS, n)
+
+    last = ITERS * CHUNKS - 1
+
+    @pl.when(left_is_far)
+    def _():
+        @pl.loop(0, CHUNKS)
+        def _(h):
+            heavy_part(1, h, False)
+
+        late_far()
+
+        @all_steps
+        def _(t, h, n):
+            pl.when(n == last)(finish_x)
+            ghost_part(t, h, held=True)
+            end_part(t + 1, h, guarded=True)
+
+    @pl.when(right_is_far)
+    def _():
+        @all_steps
+        def _(t, h, n):
+            ghost_part(t, h, sends_p=False)
+            end_part(t, h, sends_p=True)
+            heavy_part(t, h, True)
+            pl.when(n == CHUNKS - 1)(late_far)
+            pl.when(n == last)(finish_x)
+
+    @pl.when(both_near)
+    def _():
+        @all_steps
+        def _(t, h, n):
+            end_part(t, h)
+            pl.when(n == last)(finish_x)
+            ghost_part(t, h)
+            heavy_part(t, h, True)
             pl.when(n == CHUNKS - 1)(late_far)
 
     end = jnp.zeros((RHS, H), F32)
@@ -375,8 +431,8 @@
             operator,
             operator,
             operator,
-            pltpu.VMEM((CHUNKS, 2 * W, 5 * H), BF16),
-            chunk, chunk, chunk, chunk, chunk, chunk,
+            pltpu.VMEM((CHUNKS, 2, W, 4 * H), BF16),
+            chunk, chunk, chunk, chunk, chunk, chunk, chunk, chunk, chunk, chunk,
             inner, inner, inner,
             chunk,
             message, message, message, message,

time: 46.7 us -> 46.1 us (0.987)
  Pallas kernels: 44.6 us -> 44 us
    pallas_call x1, Pallas kernels: 43.6 us -> 43.1 us  [shards(): pl.pallas_call(functools.partial(kernel, far), out_shape=(block, block),...]
where the time goes in v3:
time: 46.1 us; the launch traced here: 46 us
  Pallas kernels  44 us (95%)
  between operations  1.29 us (3%)
  local copies, waits for them, and re-layouts  0.68 us (1%)
    pallas_call x1, Pallas kernels, shards(): pl.pallas_call(functools.partial(kernel, far), out_shape=(block, block),...  43.1 us
    pallas_call x1, Pallas kernels, shards(): pl.pallas_call(put_out, out_shape=(block, block), in_specs=[vmem, vmem],...  0.99 us

profile of v3, /device:TPU:24, one launch (start us, length us, event | category | flops | bytes accessed | tf_op | source)
XLA Modules:
  0.0 46.0 jit_solution(17080208296936817490)
XLA Ops:
  1.3 0.0 copy-start
  1.3 0.7 %copy-done = s32[1,1,4,256]{3,2,1,0:T(4,128)S(1)} copy-done((s32[1,1,4,256]{3,2,1,0:T(4,128)S(1)}, s32[1,1,4,256]{3,2,1,0:T(4,128)}, u32[]{:S(2)}) %copy-start) | copy-done | bytes 4120
  2.0 43.1 %feti_chebyshev.1 = (f32[1,1,4,256,128]{4,3,2,1,0:T(8,128)S(1)}, f32[1,1,4,256,128]{4,3,2,1,0:T(8,128)S(1)}) custom-call(s32[1,1]{1,0:T(1,128)S(6)} %copy.6.cnt_ref, s32[1,1,4,256]{3,2,1,0:T(4,128)S(1)} %copy-done, f32[1,1,4,512,512]{4,3,2,1,0:T(8,128)} %ops_hbm.1, f32[1,1,4,256,128]{4,3,2,1,0:T(8,128)} %gap_hbm.1), custom_call_target="tpu_custom_call" | custom-call | tf_op jit(solution)/shard_map/feti_chebyshev/pallas_call | solution.py:420
  45.0 1.0 %put_out.1 = (f32[1,1,4,256,128]{4,3,2,1,0:T(8,128)}, f32[1,1,4,256,128]{4,3,2,1,0:T(8,128)}) custom-call(f32[1,1,4,256,128]{4,3,2,1,0:T(8,128)S(1)} %get-tuple-element.4.x, f32[1,1,4,256,128]{4,3,2,1,0:T(8,128)S(1)} %get-tuple-element.5.r), custom_call_target="tpu_custom_call" | custom-call | tf_op jit(solution)/shard_map/put_out/pallas_call | solution.py:453
Async XLA Ops:
  1.3 0.7 %copy-start = (s32[1,1,4,256]{3,2,1,0:T(4,128)S(1)}, s32[1,1,4,256]{3,2,1,0:T(4,128)}, u32[]{:S(2)}) copy-start(s32[1,1,4,256]{3,2,1,0:T(4,128)} %pairs_hbm.1) | copy-start | bytes 12292

commit v4 on v3

--- a/solution.py
+++ b/solution.py
@@ -178,9 +178,10 @@
 
     pl.when(jnp.logical_not(both_near))(open_gate)
 
+    sends_block = jnp.logical_and(has_left, left_is_far)
     goes_first = lax.axis_index("grp") % 2 == 0
 
-    @pl.when(jnp.logical_and(has_left, goes_first))
+    @pl.when(jnp.logical_and(sends_block, goes_first))
     def _():
         ll_copy.start()
 
@@ -197,9 +198,20 @@
             def _():
                 p_copy(t, h).start()
 
-    def end_part(t, h, sends_p=False, guarded=False):
+    def send_q(t, h):
+        @pl.when(has_left)
+        def _():
+            @pl.when(t > 1)
+            def _():
+                q_copy(t - 1, h).wait_send()
+
+            q_copy(t, h).start()
+
+    def end_part(t, h, left_far=False, right_far=False, guarded=False):
         keep, add = chosen(KEEP, t), chosen(ADD, t)
-        partial = p_out[t - 1, h] + far_out[h]
+        partial = p_out[t - 1, h]
+        if right_far:
+            partial = partial + far_out[h]
         first = v_in[h, 0]
 
         @pl.when(jnp.logical_and(has_right, t > 1))
@@ -212,24 +224,24 @@
         def rest():
             end = keep * v_end[h] + add * r
             split = halves(end)
-            if sends_p:
+            if right_far:
                 p_out[t, h] = pg_out[h] + product(split, (w_p[0, H:], w_p[1, H:]))
                 send_p(t, h)
-            q_out[t, h] = product(halves(jnp.where(c == 1, end, first)), w_lr)
-
-            @pl.when(has_left)
-            def _():
-                @pl.when(t > 1)
-                def _():
-                    q_copy(t - 1, h).wait_send()
-
-                q_copy(t, h).start()
-
-            if not sends_p:
+            own_columns = product(halves(jnp.where(c == 1, end, first)), w_lr)
+            if left_far:
+                q_out[t, h] = own_columns
+                send_q(t, h)
+            elif right_far:
+                q_out[t, h] = own_columns + own[h]
+                send_q(t, h)
+            else:
+                own[h] = own_columns
+            if right_far:
+                far_out[h] = product(split, w_far)
+            else:
                 pl_out[h] = product(split, (w_p[0, H:], w_p[1, H:]))
             v_end[h] = end
             x_end[h] = x_end[h] + end
-            far_out[h] = product(split, w_far)
             if guarded:
                 heavy_part(t, h, False)
 
@@ -253,10 +265,11 @@
         v_in[h, j] = v
         x_in[h, j] = x_in[h, j] + v
 
-    def ghost_part(t, h, sends_p=True, held=False):
+    def ghost_part(t, h, left_far=False, right_far=False):
         keep, add = chosen(KEEP, t), chosen(ADD, t)
-        partial = q_out[t - 1, h] + own[h]
-        if held:
+        partial = q_out[t - 1, h]
+        if left_far:
+            partial = partial + own[h]
             before = before_in[h]
         else:
             before = jnp.where(c == 2, v_in[h, 0], jnp.where(c == 3, v_in[h, 1], v_in[h, 2]))
@@ -269,20 +282,24 @@
         ghost = keep * v_ghost[h] + add * r
         split = halves(ghost)
         from_left = product(halves(jnp.where(c == 1, ghost, before)), (w_p[0, :H], w_p[1, :H]))
-        if sends_p:
+        if right_far:
+            pg_out[h] = from_left
+        else:
             p_out[t, h] = from_left + pl_out[h]
+        if left_far:
+            advance(t, h, 0, product(split, (w_in[0, 0, :H], w_in[0, 1, :H])) + row_out[h])
+            send_p(t, h)
+            own[h] = product(split, w_ll)
+        elif right_far:
+            own[h] = product(split, w_ll)
+            row_out[h] = product(split, (w_in[0, 0, :H], w_in[0, 1, :H]))
         else:
-            pg_out[h] = from_left
-        y = product(split, (w_in[0, 0, :H], w_in[0, 1, :H]))
-        if held:
-            advance(t, h, 0, y + row_out[h])
-        else:
-            row_out[h] = y
+            q_out[t, h] = product(split, w_ll) + own[h]
+            send_p(t, h)
+            send_q(t, h)
+            row_out[h] = product(split, (w_in[0, 0, :H], w_in[0, 1, :H]))
         r_ghost[h] = r
         v_ghost[h] = ghost
-        if sends_p:
-            send_p(t, h)
-        own[h] = product(split, w_ll)
 
     def heavy_part(t, h, finishes):
         inner = [v_in[h, j] for j in range(3)]
@@ -311,7 +328,7 @@
     def _():
         @pl.loop(0, CHUNKS)
         def _(h):
-            end_part(1, h)
+            end_part(1, h, left_far=True)
 
     for j in range(SLOTS):
         picked = selection(pairs[j])
@@ -324,7 +341,7 @@
         if j < SLOTS - 1:
             w_in[j, 0, :H], w_in[j, 1, :H] = turned(picked, ops[j, H:, :H])
 
-    @pl.when(jnp.logical_and(has_left, jnp.logical_not(goes_first)))
+    @pl.when(jnp.logical_and(sends_block, jnp.logical_not(goes_first)))
     def _():
         ll_copy.start()
 
@@ -350,20 +367,18 @@
         def _(h):
             heavy_part(1, h, False)
 
-        late_far()
-
         @all_steps
         def _(t, h, n):
             pl.when(n == last)(finish_x)
-            ghost_part(t, h, held=True)
-            end_part(t + 1, h, guarded=True)
+            ghost_part(t, h, left_far=True)
+            end_part(t + 1, h, left_far=True, guarded=True)
 
     @pl.when(right_is_far)
     def _():
         @all_steps
         def _(t, h, n):
-            ghost_part(t, h, sends_p=False)
-            end_part(t, h, sends_p=True)
+            ghost_part(t, h, right_far=True)
+            end_part(t, h, right_far=True)
             heavy_part(t, h, True)
             pl.when(n == CHUNKS - 1)(late_far)
             pl.when(n == last)(finish_x)
@@ -376,7 +391,6 @@
             pl.when(n == last)(finish_x)
             ghost_part(t, h)
             heavy_part(t, h, True)
-            pl.when(n == CHUNKS - 1)(late_far)
 
     end = jnp.zeros((RHS, H), F32)
     for j in range(SLOTS):
@@ -387,15 +401,16 @@
         @pl.loop(0, CHUNKS)
         def _(h):
             q_copy(ITERS, h).wait_recv()
-            r_end[h] = r_end[h] - (p_out[ITERS, h] + far_out[h] + q_got[ITERS, h])
+            r_end[h] = r_end[h] - ((p_out[ITERS, h] + q_got[ITERS, h]) + jnp.where(right_is_far, far_out[h], 0.0))
 
     end = jnp.transpose(r_end[...].reshape(RHS, H))
     for j in range(SLOTS):
         out_r[0, 0, j] = jnp.where(c - 1 == j, end, out_r[0, 0, j])
 
+    pl.when(sends_block)(ll_copy.wait_send)
+
     @pl.when(has_left)
     def _():
-        ll_copy.wait_send()
         for h in range(CHUNKS):
             q_copy(ITERS, h).wait_send()
 

time: 46.1 us -> 48.5 us (1.052)
  Pallas kernels: 44 us -> 46.4 us
    pallas_call x1, Pallas kernels: 43.1 us -> 45.5 us  [shards(): pl.pallas_call(functools.partial(kernel, far), out_shape=(block, block),...]
where the time goes in v4:
time: 48.5 us; the launch traced here: 48.4 us
  Pallas kernels  46.4 us (96%)
  between operations  1.29 us (3%)
  local copies, waits for them, and re-layouts  0.68 us (1%)
    pallas_call x1, Pallas kernels, shards(): pl.pallas_call(functools.partial(kernel, far), out_shape=(block, block),...  45.5 us
    pallas_call x1, Pallas kernels, shards(): pl.pallas_call(put_out, out_shape=(block, block), in_specs=[vmem, vmem],...  0.99 us

profile of v4, /device:TPU:24, one launch (start us, length us, event | category | flops | bytes accessed | tf_op | source)
XLA Modules:
  0.0 48.4 jit_solution(14207819203040003228)
XLA Ops:
  1.3 0.0 copy-start
  1.3 0.7 %copy-done = s32[1,1,4,256]{3,2,1,0:T(4,128)S(1)} copy-done((s32[1,1,4,256]{3,2,1,0:T(4,128)S(1)}, s32[1,1,4,256]{3,2,1,0:T(4,128)}, u32[]{:S(2)}) %copy-start) | copy-done | bytes 4120
  2.0 45.5 %feti_chebyshev.1 = (f32[1,1,4,256,128]{4,3,2,1,0:T(8,128)S(1)}, f32[1,1,4,256,128]{4,3,2,1,0:T(8,128)S(1)}) custom-call(s32[1,1]{1,0:T(1,128)S(6)} %copy.6.cnt_ref, s32[1,1,4,256]{3,2,1,0:T(4,128)S(1)} %copy-done, f32[1,1,4,512,512]{4,3,2,1,0:T(8,128)} %ops_hbm.1, f32[1,1,4,256,128]{4,3,2,1,0:T(8,128)} %gap_hbm.1), custom_call_target="tpu_custom_call" | custom-call | tf_op jit(solution)/shard_map/feti_chebyshev/pallas_call | solution.py:435
  47.4 1.0 %put_out.1 = (f32[1,1,4,256,128]{4,3,2,1,0:T(8,128)}, f32[1,1,4,256,128]{4,3,2,1,0:T(8,128)}) custom-call(f32[1,1,4,256,128]{4,3,2,1,0:T(8,128)S(1)} %get-tuple-element.4.x, f32[1,1,4,256,128]{4,3,2,1,0:T(8,128)S(1)} %get-tuple-element.5.r), custom_call_target="tpu_custom_call" | custom-call | tf_op jit(solution)/shard_map/put_out/pallas_call | solution.py:468
Async XLA Ops:
  1.3 0.7 %copy-start = (s32[1,1,4,256]{3,2,1,0:T(4,128)S(1)}, s32[1,1,4,256]{3,2,1,0:T(4,128)}, u32[]{:S(2)}) copy-start(s32[1,1,4,256]{3,2,1,0:T(4,128)} %pairs_hbm.1) | copy-start | bytes 12292

commit v5 on v3

--- a/solution.py
+++ b/solution.py
@@ -176,11 +176,9 @@
     w_p[0, :H], w_p[1, :H] = turned(selection(last_pairs), ops[final_slot, H:, :H])
     w_p[0, H:], w_p[1, H:] = halves(jnp.transpose(ops[final_slot, H:, H:]))
 
-    pl.when(jnp.logical_not(both_near))(open_gate)
-
     goes_first = lax.axis_index("grp") % 2 == 0
 
-    @pl.when(jnp.logical_and(has_left, goes_first))
+    @pl.when(jnp.logical_and(both_near, goes_first))
     def _():
         ll_copy.start()
 
@@ -306,13 +304,6 @@
         for j in (1, 2):
             advance(t, h, j, product(columns(j - 1, 3), w_in.at[j]))
 
-
-    @pl.when(left_is_far)
-    def _():
-        @pl.loop(0, CHUNKS)
-        def _(h):
-            end_part(1, h)
-
     for j in range(SLOTS):
         picked = selection(pairs[j])
         if j > 0:
@@ -324,9 +315,20 @@
         if j < SLOTS - 1:
             w_in[j, 0, :H], w_in[j, 1, :H] = turned(picked, ops[j, H:, :H])
 
-    @pl.when(jnp.logical_and(has_left, jnp.logical_not(goes_first)))
-    def _():
-        ll_copy.start()
+    @pl.when(jnp.logical_not(both_near))
+    def _():
+        open_gate()
+
+        @pl.when(jnp.logical_and(has_left, goes_first))
+        def _():
+            ll_copy.start()
+
+
+    @pl.when(left_is_far)
+    def _():
+        @pl.loop(0, CHUNKS)
+        def _(h):
+            end_part(1, h)
 
     def placed(inner, end, j):
         kept = jnp.where(j < c - 1, inner, 0.0) if j < 3 else jnp.zeros_like(end)
@@ -337,6 +339,13 @@
         for j in range(SLOTS):
             out_x[0, 0, j] = placed(x_in[:, j % 3].reshape(RHS, H), end, j)
 
+    def send_later():
+        @pl.when(jnp.logical_and(has_left, jnp.logical_not(goes_first)))
+        def _():
+            ll_copy.start()
+
+    pl.when(jnp.logical_not(left_is_far))(send_later)
+
     def all_steps(body):
         @pl.loop(0, ITERS * CHUNKS)
         def _(n):
@@ -350,6 +359,7 @@
         def _(h):
             heavy_part(1, h, False)
 
+        send_later()
         late_far()
 
         @all_steps
@@ -449,7 +459,7 @@
         compiler_params=pltpu.CompilerParams(
             collective_id=0, has_side_effects=True, vmem_limit_bytes=55_200_000),
         name="feti_chebyshev",
-    )(counts, pair_rows, operators, gap)
+    )(counts, pltpu.with_memory_space_constraint(pair_rows, pltpu.HBM), operators, gap)
     return pl.pallas_call(
         put_out,
         out_shape=(block, block),

time: 46.1 us -> 45.6 us (0.989)
  local copies, waits for them, and re-layouts: 0.68 us -> 0 us
    unnamed x2 -> x0, local copies, waits for them, and re-layouts: 0.68 us -> none
where the time goes in v5:
time: 45.6 us; the launch traced here: 45.5 us
  Pallas kernels  44.2 us (97%)
  between operations  1.28 us (3%)
    pallas_call x1, Pallas kernels, shards(): pl.pallas_call(functools.partial(kernel, far), out_shape=(block, block),...  43.2 us
    pallas_call x1, Pallas kernels, shards(): pl.pallas_call(put_out, out_shape=(block, block), in_specs=[vmem, vmem],...  0.99 us

profile of v5, /device:TPU:24, one launch (start us, length us, event | category | flops | bytes accessed | tf_op | source)
XLA Modules:
  0.0 45.5 jit_solution(5661624180880038453)
XLA Ops:
  1.3 43.2 %feti_chebyshev.1 = (f32[1,1,4,256,128]{4,3,2,1,0:T(8,128)S(1)}, f32[1,1,4,256,128]{4,3,2,1,0:T(8,128)S(1)}) custom-call(s32[1,1]{1,0:T(1,128)S(6)} %copy.6.cnt_ref, s32[1,1,4,256]{3,2,1,0:T(4,128)} %pairs_hbm.1, f32[1,1,4,512,512]{4,3,2,1,0:T(8,128)} %ops_hbm.1, f32[1,1,4,256,128]{4,3,2,1,0:T(8,128)} %gap_hbm.1), custom_call_target="tpu_custom_call" | custom-call | tf_op jit(solution)/shard_map/feti_chebyshev/pallas_call | solution.py:430
  44.5 1.0 %put_out.1 = (f32[1,1,4,256,128]{4,3,2,1,0:T(8,128)}, f32[1,1,4,256,128]{4,3,2,1,0:T(8,128)}) custom-call(f32[1,1,4,256,128]{4,3,2,1,0:T(8,128)S(1)} %get-tuple-element.4.x, f32[1,1,4,256,128]{4,3,2,1,0:T(8,128)S(1)} %get-tuple-element.5.r), custom_call_target="tpu_custom_call" | custom-call | tf_op jit(solution)/shard_map/put_out/pallas_call | solution.py:463

commit v6 on v5

--- a/solution.py
+++ b/solution.py
@@ -14,6 +14,8 @@
 ITERS = 6
 CHUNKS = 2
 W = RHS // CHUNKS
+PAIR = 2
+PAIRS = CHUNKS // PAIR
 
 LOWER = 1.0
 UPPER = 14.0
@@ -178,13 +180,16 @@
 
     goes_first = lax.axis_index("grp") % 2 == 0
 
-    @pl.when(jnp.logical_and(both_near, goes_first))
-    def _():
-        ll_copy.start()
-
     def product(x, w):
         both = nn(jnp.concatenate(x, axis=0), w[0])
-        return (both[:W] + both[W:]) + nn(x[0], w[1])
+        width = both.shape[0] // 2
+        return (both[:width] + both[width:]) + nn(x[0], w[1])
+
+    def paired(g):
+        return pl.ds(g * PAIR, PAIR)
+
+    def joined(x):
+        return x.reshape(x.shape[0] * W, H)
 
     def send_p(t, h):
         @pl.when(has_right)
@@ -228,9 +233,6 @@
             v_end[h] = end
             x_end[h] = x_end[h] + end
             far_out[h] = product(split, w_far)
-            if guarded:
-                heavy_part(t, h, False)
-
         if guarded:
             pl.when(t <= ITERS)(rest)
         else:
@@ -282,27 +284,38 @@
             send_p(t, h)
         own[h] = product(split, w_ll)
 
-    def heavy_part(t, h, finishes):
-        inner = [v_in[h, j] for j in range(3)]
-        end = v_end[h]
+    def advance_pair(t, g, j, y):
+        at = paired(g)
+        r = joined(r_in[at, j]) - jnp.where(j < c - 1, y, 0.0)
+        v = chosen(KEEP, t + 1) * joined(v_in[at, j]) + chosen(ADD, t + 1) * r
+        x = joined(x_in[at, j]) + v
+        r_in[at, j] = r.reshape(PAIR, W, H)
+        v_in[at, j] = v.reshape(PAIR, W, H)
+        x_in[at, j] = x.reshape(PAIR, W, H)
+
+    def heavy_part(t, g, finishes):
+        at = paired(g)
+        inner = [joined(v_in[at, j]) for j in range(3)]
+        end = joined(v_end[at])
         if not finishes:
-            before_in[h] = jnp.where(c == 2, inner[0], jnp.where(c == 3, inner[1], inner[2]))
-        blocks = [inner[0]] + [jnp.where(c == j + 1, end, inner[j]) for j in (1, 2)] + [end]
+            before = jnp.where(c == 2, inner[0], jnp.where(c == 3, inner[1], inner[2]))
+            before_in[at] = before.reshape(PAIR, W, H)
+        blocks = [jnp.where(c == j + 1, end, inner[j]) for j in range(3)] + [end]
         for i, block in enumerate(blocks):
-            high, low = halves(jnp.where(c == 1, end, block) if i == 0 else block)
-            vb[h, 0, :, i * H:(i + 1) * H] = high
-            vb[h, 1, :, i * H:(i + 1) * H] = low
+            high, low = halves(block)
+            vb[0, :, i * H:(i + 1) * H] = high
+            vb[1, :, i * H:(i + 1) * H] = low
 
         def columns(k, width):
-            return vb[h, 0, :, k * H:(k + width) * H], vb[h, 1, :, k * H:(k + width) * H]
+            return vb[0, :, k * H:(k + width) * H], vb[1, :, k * H:(k + width) * H]
 
         y = product(columns(0, 2), (w_in[0, 0, H:], w_in[0, 1, H:]))
         if finishes:
-            advance(t, h, 0, y + row_out[h])
+            advance_pair(t, g, 0, y + joined(row_out[at]))
         else:
-            row_out[h] = y
+            row_out[at] = y.reshape(PAIR, W, H)
         for j in (1, 2):
-            advance(t, h, j, product(columns(j - 1, 3), w_in.at[j]))
+            advance_pair(t, g, j, product(columns(j - 1, 3), w_in.at[j]))
 
     for j in range(SLOTS):
         picked = selection(pairs[j])
@@ -340,53 +353,60 @@
             out_x[0, 0, j] = placed(x_in[:, j % 3].reshape(RHS, H), end, j)
 
     def send_later():
-        @pl.when(jnp.logical_and(has_left, jnp.logical_not(goes_first)))
+        @pl.when(jnp.logical_and(has_left, jnp.logical_or(both_near, jnp.logical_not(goes_first))))
         def _():
             ll_copy.start()
 
     pl.when(jnp.logical_not(left_is_far))(send_later)
 
     def all_steps(body):
-        @pl.loop(0, ITERS * CHUNKS)
+        @pl.loop(0, ITERS * PAIRS)
         def _(n):
-            body(n // CHUNKS + 1, n % CHUNKS, n)
-
-    last = ITERS * CHUNKS - 1
+            t, g = n // PAIRS + 1, n % PAIRS
+            body(t, g, [g * PAIR + k for k in range(PAIR)], n)
+
+    last = ITERS * PAIRS - 1
 
     @pl.when(left_is_far)
     def _():
-        @pl.loop(0, CHUNKS)
-        def _(h):
-            heavy_part(1, h, False)
+        @pl.loop(0, PAIRS)
+        def _(g):
+            heavy_part(1, g, False)
 
         send_later()
         late_far()
 
         @all_steps
-        def _(t, h, n):
+        def _(t, g, chunks, n):
             pl.when(n == last)(finish_x)
-            ghost_part(t, h, held=True)
-            end_part(t + 1, h, guarded=True)
+            for h in chunks:
+                ghost_part(t, h, held=True)
+                end_part(t + 1, h, guarded=True)
+            pl.when(t < ITERS)(lambda: heavy_part(t + 1, g, False))
 
     @pl.when(right_is_far)
     def _():
         @all_steps
-        def _(t, h, n):
-            ghost_part(t, h, sends_p=False)
-            end_part(t, h, sends_p=True)
-            heavy_part(t, h, True)
-            pl.when(n == CHUNKS - 1)(late_far)
+        def _(t, g, chunks, n):
+            for k, h in enumerate(chunks):
+                ghost_part(t, h, sends_p=False)
+                if k == 0:
+                    pl.when(n == PAIRS)(late_far)
+                end_part(t, h, sends_p=True)
+            heavy_part(t, g, True)
             pl.when(n == last)(finish_x)
 
     @pl.when(both_near)
     def _():
         @all_steps
-        def _(t, h, n):
-            end_part(t, h)
-            pl.when(n == last)(finish_x)
-            ghost_part(t, h)
-            heavy_part(t, h, True)
-            pl.when(n == CHUNKS - 1)(late_far)
+        def _(t, g, chunks, n):
+            for k, h in enumerate(chunks):
+                end_part(t, h)
+                if k == PAIR - 1:
+                    pl.when(n == last)(finish_x)
+                ghost_part(t, h)
+            heavy_part(t, g, True)
+            pl.when(n == PAIRS - 1)(late_far)
 
     end = jnp.zeros((RHS, H), F32)
     for j in range(SLOTS):
@@ -441,7 +461,7 @@
             operator,
             operator,
             operator,
-            pltpu.VMEM((CHUNKS, 2, W, 4 * H), BF16),
+            pltpu.VMEM((2, PAIR * W, 4 * H), BF16),
             chunk, chunk, chunk, chunk, chunk, chunk, chunk, chunk, chunk, chunk,
             inner, inner, inner,
             chunk,

time: 45.6 us -> 44.9 us (0.985)
  Pallas kernels: 44.2 us -> 43.5 us
    pallas_call x1, Pallas kernels: 43.2 us -> 42.5 us  [shards(): pl.pallas_call(functools.partial(kernel, far), out_shape=(block, block),...]
where the time goes in v6:
time: 44.9 us; the launch traced here: 44.8 us
  Pallas kernels  43.5 us (97%)
  between operations  1.28 us (3%)
    pallas_call x1, Pallas kernels, shards(): pl.pallas_call(functools.partial(kernel, far), out_shape=(block, block),...  42.5 us
    pallas_call x1, Pallas kernels, shards(): pl.pallas_call(put_out, out_shape=(block, block), in_specs=[vmem, vmem],...  0.99 us

profile of v6, /device:TPU:24, one launch (start us, length us, event | category | flops | bytes accessed | tf_op | source)
XLA Modules:
  0.0 44.8 jit_solution(8536578018521213206)
XLA Ops:
  1.3 42.5 %feti_chebyshev.1 = (f32[1,1,4,256,128]{4,3,2,1,0:T(8,128)S(1)}, f32[1,1,4,256,128]{4,3,2,1,0:T(8,128)S(1)}) custom-call(s32[1,1]{1,0:T(1,128)S(6)} %copy.6.cnt_ref, s32[1,1,4,256]{3,2,1,0:T(4,128)} %pairs_hbm.1, f32[1,1,4,512,512]{4,3,2,1,0:T(8,128)} %ops_hbm.1, f32[1,1,4,256,128]{4,3,2,1,0:T(8,128)} %gap_hbm.1), custom_call_target="tpu_custom_call" | custom-call | tf_op jit(solution)/shard_map/feti_chebyshev/pallas_call | solution.py:450
  43.8 1.0 %put_out.1 = (f32[1,1,4,256,128]{4,3,2,1,0:T(8,128)}, f32[1,1,4,256,128]{4,3,2,1,0:T(8,128)}) custom-call(f32[1,1,4,256,128]{4,3,2,1,0:T(8,128)S(1)} %get-tuple-element.4.x, f32[1,1,4,256,128]{4,3,2,1,0:T(8,128)S(1)} %get-tuple-element.5.r), custom_call_target="tpu_custom_call" | custom-call | tf_op jit(solution)/shard_map/put_out/pallas_call | solution.py:483

commit v7 on v6

--- a/solution.py
+++ b/solution.py
@@ -372,6 +372,10 @@
         @pl.loop(0, PAIRS)
         def _(g):
             heavy_part(1, g, False)
+
+        @pl.when(jnp.logical_not(goes_first))
+        def _():
+            pl.delay(1500)
 
         send_later()
         late_far()

time: 44.9 us -> 44.5 us (level)
  no operation moved by 1% of the time
where the time goes in v7:
time: 44.5 us; the launch traced here: 44.4 us
  Pallas kernels  43.1 us (97%)
  between operations  1.28 us (3%)
    pallas_call x1, Pallas kernels, shards(): pl.pallas_call(functools.partial(kernel, far), out_shape=(block, block),...  42.1 us
    pallas_call x1, Pallas kernels, shards(): pl.pallas_call(put_out, out_shape=(block, block), in_specs=[vmem, vmem],...  0.99 us

profile of v7, /device:TPU:24, one launch (start us, length us, event | category | flops | bytes accessed | tf_op | source)
XLA Modules:
  0.0 44.4 jit_solution(1180271572274468111)
XLA Ops:
  1.3 42.1 %feti_chebyshev.1 = (f32[1,1,4,256,128]{4,3,2,1,0:T(8,128)S(1)}, f32[1,1,4,256,128]{4,3,2,1,0:T(8,128)S(1)}) custom-call(s32[1,1]{1,0:T(1,128)S(6)} %copy.6.cnt_ref, s32[1,1,4,256]{3,2,1,0:T(4,128)} %pairs_hbm.1, f32[1,1,4,512,512]{4,3,2,1,0:T(8,128)} %ops_hbm.1, f32[1,1,4,256,128]{4,3,2,1,0:T(8,128)} %gap_hbm.1), custom_call_target="tpu_custom_call" | custom-call | tf_op jit(solution)/shard_map/feti_chebyshev/pallas_call | solution.py:454
  43.4 1.0 %put_out.1 = (f32[1,1,4,256,128]{4,3,2,1,0:T(8,128)}, f32[1,1,4,256,128]{4,3,2,1,0:T(8,128)}) custom-call(f32[1,1,4,256,128]{4,3,2,1,0:T(8,128)S(1)} %get-tuple-element.4.x, f32[1,1,4,256,128]{4,3,2,1,0:T(8,128)S(1)} %get-tuple-element.5.r), custom_call_target="tpu_custom_call" | custom-call | tf_op jit(solution)/shard_map/put_out/pallas_call | solution.py:487
